TPU v7x, 32 devices: a whole 2x2x4 slice. The times are simulated.
32 devices in a mesh: mem: 4 (over y, core), sub: 8 (over z, x).
Axes of the slice: x: 2, y: 2, z: 4, core: 2. Of those that a mesh axis runs over, the one named last changes fastest.
Arguments:
- prior_sample_array: float32 [80, 8, 24, 512], P('mem', 'sub'), may hold values from -6 to 6
- courant_x: float32 [8, 512], P('sub'), may hold values from -0.3 to 0.3
- courant_y: float32 [8, 512], P('sub'), may hold values from -0.3 to 0.3
- diffusion: float32 [8, 512], P('sub'), may hold values from 0.02 to 0.09
- obs_cell: int32 [4, 128], replicated, may hold values from 0 to 4095
- obs_value: float32 [4, 128], replicated, may hold values from -6 to 6
- obs_error: float32 [4, 128], replicated, may hold values from 0.2 to 1
- obs_weight: float32 [4, 128, 24], replicated, may hold values from -1.25 to 1.25
- taper_radius: float32 [4, 128], replicated, may hold values from 64 to 256
Outputs:
- analysis: float32 [80, 8, 24, 512], P(None, 'sub', None, 'mem')
All inputs are finite; a program needn't handle non-finite values.
Results may differ from a plain program's by a relative error of at most 0.0003.
Values sent between devices are 32-bit elements; how exact they have to be, the bound alone decides.
No kernel may reach another device: no remote copies, remote signals or barrier semaphores. Data moves between devices by JAX's collectives and lax.ppermute only.
A program may use at most 64 MiB of HBM per device.

v0:
```python
import jax
import jax.numpy as jnp
from jax import lax
from jax.sharding import PartitionSpec as P

highest = lax.Precision.HIGHEST


def padded_2(shard, sides, width):
    for axis, dim in sides:
        size, length = (lax.axis_size(axis), shard.shape[dim])
        up = [(i, (i + 1) % size) for i in range(size - 1)]
        down = [(j, i) for i, j in up]
        last = lax.slice_in_dim(shard, length - width, length, axis=dim)
        first = lax.slice_in_dim(shard, 0, width, axis=dim)
        before = lax.ppermute(last, axis, up)
        after = lax.ppermute(first, axis, down)
        shard = jnp.concatenate([before, shard, after], axis=dim)
    return shard


def gaspari(delta_row, delta_col, cutoff_radius, width):
    cyclic_shifted = (delta_col + width // 2) % width - width // 2
    row_dist = delta_row.astype(jnp.float32)
    col_dist = cyclic_shifted.astype(jnp.float32)
    ratio = jnp.sqrt(row_dist * row_dist + col_dist * col_dist) / cutoff_radius
    inner = (((-0.25 * ratio + 0.5) * ratio + 0.625) * ratio - 5.0 / 3.0) * ratio * ratio + 1.0
    bounded = jnp.maximum(ratio, 1.0)
    outer = (
        ((((ratio / 12.0 - 0.5) * ratio + 0.625) * ratio + 5.0 / 3.0) * ratio - 5.0) * ratio
        + 4.0
        - 2.0 / (3.0 * bounded)
    )
    return jnp.where(ratio <= 1.0, inner, jnp.where(ratio < 2.0, outer, 0.0))


def carried_quantity(
    center,
    west_cells,
    east_cells,
    north_cells,
    southern_neighbours,
    flow_x,
    meridional_velocity,
    mixing,
):
    result = (
        center
        - jnp.maximum(flow_x, 0.0) * (center - west_cells)
        - jnp.minimum(flow_x, 0.0) * (east_cells - center)
    )
    result = (
        result
        - jnp.maximum(meridional_velocity, 0.0) * (center - southern_neighbours)
        - jnp.minimum(meridional_velocity, 0.0) * (north_cells - center)
    )
    return result + mixing * (
        east_cells + west_cells + north_cells + southern_neighbours - 4.0 * center
    )


def obs_factors(obs_prior, obs_value, obs_error):
    members = obs_prior.shape[1]
    average = jnp.mean(obs_prior, axis=1)
    anomaly = obs_prior - average[:, None]
    covariance = jnp.dot(anomaly, anomaly.T, precision=highest) / (members - 1) + jnp.diag(
        obs_error
    )
    factor = jnp.linalg.cholesky(covariance)
    innovation = (obs_value - average)[:, None]
    midpoint_values = lax.linalg.triangular_solve(factor, innovation, left_side=True, lower=True)
    solved = lax.linalg.triangular_solve(
        factor, midpoint_values, left_side=True, lower=True, transpose_a=True
    )
    shifted = factor + jnp.diag(jnp.sqrt(obs_error))
    reduced = lax.linalg.triangular_solve(shifted, anomaly, left_side=True, lower=True)
    squared = lax.linalg.triangular_solve(
        factor, reduced, left_side=True, lower=True, transpose_a=True
    )
    return (anomaly, solved - squared)


def local_prior(existing_grid_values, obs_rows, obs_cols, weights, row_start, col_start):
    rows_dev = existing_grid_values.shape[1]
    cols_dev = existing_grid_values.shape[3]
    local_rows = obs_rows - row_start
    local_cols = obs_cols - col_start
    owned = (
        (local_rows >= 0) & (local_rows < rows_dev) & (local_cols >= 0) & (local_cols < cols_dev)
    )
    picked = existing_grid_values[
        :, jnp.clip(local_rows, 0, rows_dev - 1), :, jnp.clip(local_cols, 0, cols_dev - 1)
    ]
    values = jnp.einsum("kmc,kc->km", picked, weights, precision=highest)
    return jnp.where(owned[:, None], values, 0.0)


def apply_update(existing_grid_values, obs_anomaly, coeffs, taper_cells, members):
    average = jnp.mean(existing_grid_values, axis=0)
    anomaly = existing_grid_values - average[None]
    cross_cov = jnp.einsum("mrcx,km->rcxk", anomaly, obs_anomaly, precision=highest) / (members - 1)
    gain = cross_cov * taper_cells[:, None, :, :]
    return existing_grid_values + jnp.einsum("rcxk,km->mrcx", gain, coeffs, precision=highest)


def shards(
    prior_sample_array,
    courant_x,
    courant_y,
    diffusion,
    obs_cell,
    obs_value,
    obs_error,
    obs_weight,
    taper_radius,
):
    width = courant_x.shape[1]
    rows_dev = prior_sample_array.shape[1]
    cols_dev = width // lax.axis_size("mem")
    members = prior_sample_array.shape[0] * lax.axis_size("mem")
    col_start = lax.axis_index("mem") * cols_dev
    row_start = lax.axis_index("sub") * rows_dev
    padded = padded_2(prior_sample_array, (("sub", 1),), 1)
    propagated_grids = carried_quantity(
        prior_sample_array,
        jnp.roll(prior_sample_array, 1, axis=3),
        jnp.roll(prior_sample_array, -1, axis=3),
        padded[:, 2:],
        padded[:, :-2],
        courant_x[:, None, :],
        courant_y[:, None, :],
        diffusion[:, None, :],
    )
    existing_grid_values = lax.all_to_all(
        propagated_grids, "mem", split_axis=3, concat_axis=0, tiled=True
    )
    row_ids = row_start + jnp.arange(rows_dev, dtype=jnp.int32)
    col_ids = col_start + jnp.arange(cols_dev, dtype=jnp.int32)
    obs_rows = obs_cell // width
    obs_cols = obs_cell % width
    batches = obs_cell.shape[0]

    def taper_cells(batch_index):
        return gaspari(
            row_ids[:, None, None] - obs_rows[batch_index][None, None, :],
            col_ids[None, :, None] - obs_cols[batch_index][None, None, :],
            taper_radius[batch_index][None, None, :],
            width,
        )

    for batch_index in range(batches):
        obs_prior = lax.psum(
            local_prior(
                existing_grid_values,
                obs_rows[batch_index],
                obs_cols[batch_index],
                obs_weight[batch_index],
                row_start,
                col_start,
            ),
            ("mem", "sub"),
        )
        obs_anomaly, coeffs = obs_factors(obs_prior, obs_value[batch_index], obs_error[batch_index])
        existing_grid_values = apply_update(
            existing_grid_values, obs_anomaly, coeffs, taper_cells(batch_index), members
        )
    return existing_grid_values


def solution(mesh):
    return jax.shard_map(
        shards,
        mesh=mesh,
        in_specs=(
            P("mem", "sub", None, None),
            P("sub", None),
            P("sub", None),
            P("sub", None),
            P(),
            P(),
            P(),
            P(),
            P(),
        ),
        out_specs=P(None, "sub", None, "mem"),
        check_vma=False,
    )
```

profile of v0, /device:TPU:0, one launch (start us, length us, event | category | flops | bytes accessed | tf_op | source)
XLA Modules:
  0.0 428.5 jit_solution(3687478982285887635)
XLA Ops:
  0.0 5.9 %collective-permute-start = (f32[20,1,24,512]{3,2,1,0:T(8,128)}, f32[20,1,24,512]{3,2,1,0:T(8,128)}, u32[]{:S(2)}, u32[]{:S(2)}) collective-permute-start(f32[20,1,24,512]{3,2,1,0:T(8,128)} %param.18), channel_id=1, source_target_pairs={{0,1},{1,2},{2,3},{3,4},{4,5},{5,6},{6,7},{8,9},{9,10},{10,11},{11... | collective-permute-start | bytes 2949128 | tf_op jit(solution)/shard_map/ppermute | solution.py:16
  14.5 32.9 %collective-permute-done = f32[20,1,24,512]{3,2,1,0:T(8,128)} collective-permute-done((f32[20,1,24,512]{3,2,1,0:T(8,128)}, f32[20,1,24,512]{3,2,1,0:T(8,128)}, u32[]{:S(2)}, u32[]{:S(2)}) %collective-permute-start) | collective-permute-done | bytes 983072 | tf_op jit(solution)/shard_map/ppermute | solution.py:16
  50.7 4.3 copy.87
  54.9 6.5 %reshape.1524 = f32[4,1,61440]{2,1,0:T(1,128)} reshape(f32[512,1,20,24]{3,2,1,0:T(8,128)} %bitcast.330) | data formatting | bytes 1966080
  61.5 4.1 all-to-all-start
  68.4 10.9 %all-to-all-done = f32[4,1,61440]{2,1,0:T(1,128)S(1)} async-done(((f32[4,1,61440]{2,1,0:T(1,128)}), f32[4,1,61440]{2,1,0:T(1,128)S(1)}, u32[]{:S(2)}, u32[]{:S(2)}) %all-to-all-start) | async-done | bytes 983072 | tf_op jit(solution)/shard_map/all_to_all | solution.py:134
  83.3 6.0 %reshape.1525 = f32[512,1,20,24]{3,2,1,0:T(8,128)} reshape(f32[4,61440]{1,0:T(4,128)S(1)} %reduce.20) | data formatting | bytes 1966080
  89.4 5.6 %copy.88 = f32[20,1,24,512]{3,1,2,0:T(1,128)S(1)} copy(f32[20,1,24,512]{2,0,1,3:T(8,128)} %bitcast.331) | data formatting | bytes 1966080 | tf_op jit(solution)/shard_map/all_to_all | solution.py:134
  99.2 41.8 %psum.28 = f32[128,80]{0,1:T(8,128)S(1)} all-reduce(f32[128,80]{0,1:T(8,128)S(1)} %broadcast_select_fusion.3), channel_id=1, replica_groups=mesh['mem'=4,'sub'=8] {'mem','sub'}, use_global_device_ids=true, to_apply=%region_0.1 | all-reduce | flops 10240 | bytes 81920 | tf_op jit(solution)/shard_map/psum | solution.py:152
  143.0 11.7 %cholesky.74 = f32[128,128]{1,0:T(8,128)S(1)} custom-call(f32[128,128]{1,0:T(8,128)S(1)} %copy.93), custom_call_target="Cholesky" | custom-call | tf_op jit(solution)/shard_map/jit(cholesky)/cholesky | solution.py:69
  156.1 9.8 %custom-call.36 = f32[1,128,128]{1,2,0:T(8,128)S(1)} custom-call(f32[1,128,128]{2,1,0:T(8,128)S(1)} %get-tuple-element.21), custom_call_target="InvertDiagBlocksLowerTriangular" | custom-call | tf_op jit(solution)/shard_map/triangular_solve/custom-call.3 | solution.py:76
  166.1 9.8 %custom-call.35 = f32[1,128,128]{1,2,0:T(8,128)S(1)} custom-call(f32[1,128,128]{2,1,0:T(8,128)S(1)} %get-tuple-element.20), custom_call_target="InvertDiagBlocksLowerTriangular" | custom-call | tf_op jit(solution)/shard_map/triangular_solve/custom-call.2 | solution.py:72
  184.5 40.4 %psum.29 = f32[128,80]{0,1:T(8,128)S(1)} all-reduce(f32[128,80]{0,1:T(8,128)S(1)} %broadcast_select_fusion.2), channel_id=1, replica_groups=mesh['mem'=4,'sub'=8] {'mem','sub'}, use_global_device_ids=true, to_apply=%region_5.11 | all-reduce | flops 10240 | bytes 81920 | tf_op jit(solution)/shard_map/psum | solution.py:152
  225.5 11.7 %cholesky.85 = f32[128,128]{1,0:T(8,128)S(1)} custom-call(f32[128,128]{1,0:T(8,128)S(1)} %copy.98), custom_call_target="Cholesky" | custom-call | tf_op jit(solution)/shard_map/jit(cholesky)/cholesky | solution.py:69
  238.7 9.8 %custom-call.40 = f32[1,128,128]{1,2,0:T(8,128)S(1)} custom-call(f32[1,128,128]{2,1,0:T(8,128)S(1)} %get-tuple-element.19), custom_call_target="InvertDiagBlocksLowerTriangular" | custom-call | tf_op jit(solution)/shard_map/triangular_solve/custom-call.3 | solution.py:76
  248.7 9.8 %custom-call.39 = f32[1,128,128]{1,2,0:T(8,128)S(1)} custom-call(f32[1,128,128]{2,1,0:T(8,128)S(1)} %get-tuple-element.18), custom_call_target="InvertDiagBlocksLowerTriangular" | custom-call | tf_op jit(solution)/shard_map/triangular_solve/custom-call.2 | solution.py:72
  266.2 40.3 %psum.30 = f32[128,80]{0,1:T(8,128)S(1)} all-reduce(f32[128,80]{0,1:T(8,128)S(1)} %broadcast_select_fusion.1), channel_id=1, replica_groups=mesh['mem'=4,'sub'=8] {'mem','sub'}, use_global_device_ids=true, to_apply=%region_8.14 | all-reduce | flops 10240 | bytes 81920 | tf_op jit(solution)/shard_map/psum | solution.py:152
  307.1 11.7 %cholesky.96 = f32[128,128]{1,0:T(8,128)S(1)} custom-call(f32[128,128]{1,0:T(8,128)S(1)} %copy.101), custom_call_target="Cholesky" | custom-call | tf_op jit(solution)/shard_map/jit(cholesky)/cholesky | solution.py:69
  320.2 9.8 %custom-call.44 = f32[1,128,128]{1,2,0:T(8,128)S(1)} custom-call(f32[1,128,128]{2,1,0:T(8,128)S(1)} %get-tuple-element.17), custom_call_target="InvertDiagBlocksLowerTriangular" | custom-call | tf_op jit(solution)/shard_map/triangular_solve/custom-call.3 | solution.py:76
  330.2 9.8 %custom-call.43 = f32[1,128,128]{1,2,0:T(8,128)S(1)} custom-call(f32[1,128,128]{2,1,0:T(8,128)S(1)} %get-tuple-element.16), custom_call_target="InvertDiagBlocksLowerTriangular" | custom-call | tf_op jit(solution)/shard_map/triangular_solve/custom-call.2 | solution.py:72
  347.7 40.6 %psum.31 = f32[128,80]{0,1:T(8,128)S(1)} all-reduce(f32[128,80]{0,1:T(8,128)S(1)} %broadcast_select_fusion), channel_id=1, replica_groups=mesh['mem'=4,'sub'=8] {'mem','sub'}, use_global_device_ids=true, to_apply=%region_11.17 | all-reduce | flops 10240 | bytes 81920 | tf_op jit(solution)/shard_map/psum | solution.py:152
  388.9 11.7 %cholesky.107 = f32[128,128]{1,0:T(8,128)S(1)} custom-call(f32[128,128]{1,0:T(8,128)S(1)} %copy.104), custom_call_target="Cholesky" | custom-call | tf_op jit(solution)/shard_map/jit(cholesky)/cholesky | solution.py:69
  402.2 9.8 %custom-call.48 = f32[1,128,128]{1,2,0:T(8,128)S(1)} custom-call(f32[1,128,128]{2,1,0:T(8,128)S(1)} %get-tuple-element.15), custom_call_target="InvertDiagBlocksLowerTriangular" | custom-call | tf_op jit(solution)/shard_map/triangular_solve/custom-call.3 | solution.py:76
  412.2 9.8 %custom-call.47 = f32[1,128,128]{1,2,0:T(8,128)S(1)} custom-call(f32[1,128,128]{2,1,0:T(8,128)S(1)} %get-tuple-element.14), custom_call_target="InvertDiagBlocksLowerTriangular" | custom-call | tf_op jit(solution)/shard_map/triangular_solve/custom-call.2 | solution.py:72
  (169 shorter events, 62.6 us)
Async XLA Ops:
  0.0 14.1 %copy-start.8 = (f32[20,1,24,512]{3,2,1,0:T(8,128)S(1)}, f32[20,1,24,512]{3,2,1,0:T(8,128)}, u32[]{:S(2)}) copy-start(f32[20,1,24,512]{3,2,1,0:T(8,128)} %param.18) | copy-start | bytes 2949124
  0.0 47.4 %collective-permute-start = (f32[20,1,24,512]{3,2,1,0:T(8,128)}, f32[20,1,24,512]{3,2,1,0:T(8,128)}, u32[]{:S(2)}, u32[]{:S(2)}) collective-permute-start(f32[20,1,24,512]{3,2,1,0:T(8,128)} %param.18), channel_id=1, source_target_pairs={{0,1},{1,2},{2,3},{3,4},{4,5},{5,6},{6,7},{8,9},{9,10},{10,11},{11... | collective-permute-start | bytes 2949128 | tf_op jit(solution)/shard_map/ppermute | solution.py:16
  5.9 41.4 %collective-permute-start.1 = (f32[20,1,24,512]{3,2,1,0:T(8,128)}, f32[20,1,24,512]{3,2,1,0:T(8,128)S(1)}, u32[]{:S(2)}, u32[]{:S(2)}) collective-permute-start(f32[20,1,24,512]{3,2,1,0:T(8,128)} %param.18), channel_id=1, source_target_pairs={{1,0},{2,1},{3,2},{4,3},{5,4},{6,5},{7,6},{9,8},{10,9},{11,10},{12... | collective-permute-start | bytes 2949128 | tf_op jit(solution)/shard_map/ppermute | solution.py:17
  14.1 34.2 %copy-start.15 = (f32[1,512]{1,0:T(1,128)S(1)}, f32[1,512]{1,0:T(1,128)}, u32[]{:S(2)}) copy-start(f32[1,512]{1,0:T(1,128)} %param.21) | copy-start | bytes 6148
  61.5 6.4 %copy-start.28 = (f32[4,128]{1,0:T(4,128)S(1)}, f32[4,128]{1,0:T(4,128)}, u32[]{:S(2)}) copy-start(f32[4,128]{1,0:T(4,128)} %param.26) | copy-start | bytes 6148
  61.5 17.8 %all-to-all-start = ((f32[4,1,61440]{2,1,0:T(1,128)}), f32[4,1,61440]{2,1,0:T(1,128)S(1)}, u32[]{:S(2)}, u32[]{:S(2)}) async-start(f32[4,1,61440]{2,1,0:T(1,128)} %reshape.1524), calls=%async_computation | async-start | bytes 1966080 | tf_op jit(solution)/shard_map/all_to_all | solution.py:134
  94.9 0.9 copy-start.9
  95.9 1.0 copy-start.6
  97.7 1.5 copy-start.19
  97.7 44.8 %copy-start.27 = (f32[128]{0:T(128)S(1)}, f32[128]{0:T(128)}, u32[]{:S(2)}) copy-start(f32[128]{0:T(128)} %get-tuple-element.52) | copy-start | bytes 1540
  97.7 57.7 %copy-start.26 = (f32[128]{0:T(128)S(1)}, f32[128]{0:T(128)}, u32[]{:S(2)}) copy-start(f32[128]{0:T(128)} %get-tuple-element.49) | copy-start | bytes 1540
  99.1 76.8 %copy-start.13 = (f32[4,128]{1,0:T(4,128)S(1)}, f32[4,128]{1,0:T(4,128)}, u32[]{:S(2)}) copy-start(f32[4,128]{1,0:T(4,128)} %param.23) | copy-start | bytes 6148
  99.1 77.2 %copy-start.7 = (f32[4,20,1,24,128]{4,3,1,0,2:T(8,128)S(1)}, f32[4,20,1,24,128]{4,3,1,0,2:T(8,128)}, u32[]{:S(2)}) copy-start(f32[4,20,1,24,128]{4,3,1,0,2:T(8,128)} %copy-done.6) | copy-start | bytes 2949124
  183.9 41.1 %copy-start.25 = (f32[128]{0:T(128)S(1)}, f32[128]{0:T(128)}, u32[]{:S(2)}) copy-start(f32[128]{0:T(128)} %get-tuple-element.51) | copy-start | bytes 1540
  183.9 54.1 %copy-start.24 = (f32[128]{0:T(128)S(1)}, f32[128]{0:T(128)}, u32[]{:S(2)}) copy-start(f32[128]{0:T(128)} %get-tuple-element.48) | copy-start | bytes 1540
  183.9 75.0 %copy-start.12 = (f32[24,128]{1,0:T(8,128)S(1)}, f32[24,128]{1,0:T(8,128)}, u32[]{:S(2)}) copy-start(f32[24,128]{1,0:T(8,128)} %get-tuple-element.64) | copy-start | bytes 36868
  183.9 75.0 %copy-start.3 = (f32[80,24,128]{2,0,1:T(8,128)S(1)}, f32[80,24,128]{2,0,1:T(8,128)}, u32[]{:S(2)}) copy-start(f32[80,24,128]{2,0,1:T(8,128)} %copy-done.2) | copy-start | bytes 2949124
  265.5 41.0 %copy-start.23 = (f32[128]{0:T(128)S(1)}, f32[128]{0:T(128)}, u32[]{:S(2)}) copy-start(f32[128]{0:T(128)} %get-tuple-element.53) | copy-start | bytes 1540
  265.5 54.0 %copy-start.22 = (f32[128]{0:T(128)S(1)}, f32[128]{0:T(128)}, u32[]{:S(2)}) copy-start(f32[128]{0:T(128)} %get-tuple-element.47) | copy-start | bytes 1540
  265.5 74.9 %copy-start.5 = (f32[80,24,128]{2,0,1:T(8,128)S(1)}, f32[80,24,128]{2,0,1:T(8,128)}, u32[]{:S(2)}) copy-start(f32[80,24,128]{2,0,1:T(8,128)} %copy-done.4) | copy-start | bytes 2949124
  347.1 41.3 %copy-start.21 = (f32[128]{0:T(128)S(1)}, f32[128]{0:T(128)}, u32[]{:S(2)}) copy-start(f32[128]{0:T(128)} %get-tuple-element.50) | copy-start | bytes 1540
  347.1 54.3 %copy-start.20 = (f32[128]{0:T(128)S(1)}, f32[128]{0:T(128)}, u32[]{:S(2)}) copy-start(f32[128]{0:T(128)} %get-tuple-element.46) | copy-start | bytes 1540
  347.1 74.9 %copy-start.14 = (f32[4,128]{1,0:T(4,128)S(1)}, f32[4,128]{1,0:T(4,128)}, u32[]{:S(2)}) copy-start(f32[4,128]{1,0:T(4,128)} %param.23) | copy-start | bytes 6148
  347.1 75.3 %copy-start.1 = (f32[80,24,128]{2,0,1:T(8,128)S(1)}, f32[80,24,128]{2,0,1:T(8,128)}, u32[]{:S(2)}) copy-start(f32[80,24,128]{2,0,1:T(8,128)} %copy-done) | copy-start | bytes 2949124
  (8 other events, 6.6 us)
where the time goes:
time: 432 us; the launch traced here: 428 us
  blocking collectives  163 us (38%)
  other arithmetic  145 us (34%)
  waiting for transfers between devices  43.8 us (10%)
  local copies, waits for them, and re-layouts  41.1 us (10%)
  matrix products  23.1 us (5%)
  starting transfers between devices  11.3 us (3%)
    psum x4, blocking collectives, shards(): lax.psum(local_prior(existing_grid_values, obs_rows[batch_index], obs_col...  163 us
    another operation x12, other arithmetic, obs_factors(): factor = jnp.linalg.cholesky(covariance)  49.7 us
    another operation x8, other arithmetic, obs_factors(): lax.linalg.triangular_solve(factor, midpoint_values, left_side=True, lowe...  42.2 us
    another operation x4, other arithmetic, obs_factors(): lax.linalg.triangular_solve(shifted, anomaly, left_side=True, lower=True)  39.2 us
    ppermute x1, waiting for transfers between devices, padded_2(): before = lax.ppermute(last, axis, up)  32.9 us
    unnamed x64, local copies, waits for them, and re-layouts  17.7 us
    all_to_all x1, waiting for transfers between devices, shards(): lax.all_to_all(propagated_grids, 'mem', split_axis=3, concat_axis=0, tile...  10.9 us
    dot_general x4, matrix products, apply_update(): jnp.einsum('mrcx,km->rcxk', anomaly, obs_anomaly, precision=highest)  10.5 us
  transfers between devices with their start and end apart: 3, of which 2 were waited for; matrix products, arithmetic and copies ran while one was open for 2% of the time, Pallas kernels for 0%

commit v1 on v0

--- a/solution.py
+++ b/solution.py
@@ -4,6 +4,18 @@
 from jax.sharding import PartitionSpec as P
 
 highest = lax.Precision.HIGHEST
+
+
+def split_up(array, dim, length):
+    lengths = array.shape
+    blocks = array.reshape(*lengths[:dim], length, lengths[dim] // length, *lengths[dim + 1 :])
+    return jnp.moveaxis(blocks, dim, 0)
+
+
+def joined_along(pieces, dim):
+    dims = list(pieces.shape[1:])
+    dims[dim] *= pieces.shape[0]
+    return jnp.moveaxis(pieces, 0, dim).reshape(dims)
 
 
 def padded_2(shard, sides, width):
@@ -131,9 +143,14 @@
         courant_y[:, None, :],
         diffusion[:, None, :],
     )
-    existing_grid_values = lax.all_to_all(
-        propagated_grids, "mem", split_axis=3, concat_axis=0, tiled=True
-    )
+    size_2, mine = (lax.axis_size("mem"), lax.axis_index("mem"))
+    tiles = split_up(propagated_grids, 3, size_2)
+    finished = [tiles[mine]]
+    for step in range(1, size_2):
+        sent = tiles[mine ^ step]
+        finished.append(lax.ppermute(sent, "mem", [(i_2, i_2 ^ step) for i_2 in range(size_2)]))
+    tiles = jnp.stack(finished)[mine ^ jnp.arange(size_2)]
+    existing_grid_values = joined_along(tiles, 0)
     row_ids = row_start + jnp.arange(rows_dev, dtype=jnp.int32)
     col_ids = col_start + jnp.arange(cols_dev, dtype=jnp.int32)
     obs_rows = obs_cell // width

time: 432 us -> 404 us (0.935)
  local copies, waits for them, and re-layouts: 41.1 us -> 18.2 us
    unnamed x64 -> x56, local copies, waits for them, and re-layouts: 17.7 us -> 3.26 us
    all_to_all x1 -> x0, waiting for transfers between devices: 10.9 us -> none  [shards(): lax.all_to_all(propagated_grids, 'mem', split_axis=3, concat_axis=0, tile...]
    ppermute x0 -> x3, waiting for transfers between devices: none -> 9.48 us  [shards(): lax.ppermute(sent, 'mem', [(i_2, i_2 ^ step) for i_2 in range(size_2)])]
    all_to_all x4 -> x0, local copies, waits for them, and re-layouts: 6.76 us -> none  [shards(): lax.all_to_all(propagated_grids, 'mem', split_axis=3, concat_axis=0, tile...]
  transfers between devices with their start and end apart: 3 -> 5, of which waited for: 2 -> 3; matrix products, arithmetic and copies ran while one was open for 2% -> 3% of each run, Pallas kernels for 0% -> 0%
where the time goes in v1:
time: 404 us; the launch traced here: 398 us
  blocking collectives  164 us (41%)
  other arithmetic  141 us (35%)
  waiting for transfers between devices  40.9 us (10%)
  matrix products  23.2 us (6%)
  local copies, waits for them, and re-layouts  18.2 us (5%)
  starting transfers between devices  9.13 us (2%)
    psum x4, blocking collectives, shards(): lax.psum(local_prior(existing_grid_values, obs_rows[batch_index], obs_col...  164 us
    another operation x12, other arithmetic, obs_factors(): factor = jnp.linalg.cholesky(covariance)  49.7 us
    another operation x8, other arithmetic, obs_factors(): lax.linalg.triangular_solve(factor, midpoint_values, left_side=True, lowe...  42.1 us
    another operation x4, other arithmetic, obs_factors(): lax.linalg.triangular_solve(shifted, anomaly, left_side=True, lower=True)  39.2 us
    ppermute x1, waiting for transfers between devices, padded_2(): before = lax.ppermute(last, axis, up)  31.4 us
    dot_general x4, matrix products, apply_update(): jnp.einsum('mrcx,km->rcxk', anomaly, obs_anomaly, precision=highest)  10.5 us
    ppermute x3, waiting for transfers between devices, shards(): lax.ppermute(sent, 'mem', [(i_2, i_2 ^ step) for i_2 in range(size_2)])  9.48 us
    dot_general x4, matrix products, apply_update(): jnp.einsum('rcxk,km->mrcx', gain, coeffs, precision=highest)  8.39 us
  transfers between devices with their start and end apart: 5, of which 3 were waited for; matrix products, arithmetic and copies ran while one was open for 3% of the time, Pallas kernels for 0%

profile of v1, /device:TPU:0, one launch (start us, length us, event | category | flops | bytes accessed | tf_op | source)
XLA Modules:
  0.0 397.8 jit_solution(13758184502898599711)
XLA Ops:
  0.0 5.9 %collective-permute-start = (f32[20,1,24,512]{3,2,1,0:T(8,128)}, f32[20,1,24,512]{3,2,1,0:T(8,128)}, u32[]{:S(2)}, u32[]{:S(2)}) collective-permute-start(f32[20,1,24,512]{3,2,1,0:T(8,128)} %param.18), channel_id=1, source_target_pairs={{0,1},{1,2},{2,3},{3,4},{4,5},{5,6},{6,7},{8,9},{9,10},{10,11},{11... | collective-permute-start | bytes 2949128 | tf_op jit(solution)/shard_map/ppermute | solution.py:28
  15.9 31.4 %collective-permute-done = f32[20,1,24,512]{3,2,1,0:T(8,128)} collective-permute-done((f32[20,1,24,512]{3,2,1,0:T(8,128)}, f32[20,1,24,512]{3,2,1,0:T(8,128)}, u32[]{:S(2)}, u32[]{:S(2)}) %collective-permute-start) | collective-permute-done | bytes 983072 | tf_op jit(solution)/shard_map/ppermute | solution.py:28
  55.2 4.1 %collective-permute-done.4 = f32[20,1,24,128]{3,2,0,1:T(8,128)S(1)} collective-permute-done((f32[20,1,24,128]{3,2,0,1:T(8,128)S(1)}, f32[20,1,24,128]{3,2,0,1:T(8,128)S(1)}, u32[]{:S(2)}, u32[]{:S(2)}) %collective-permute-start.4) | collective-permute-done | bytes 245792 | tf_op jit(solution)/shard_map/ppermute | solution.py:151
  59.3 5.3 %collective-permute-done.3 = f32[20,1,24,128]{3,2,0,1:T(8,128)S(1)} collective-permute-done((f32[20,1,24,128]{3,2,0,1:T(8,128)S(1)}, f32[20,1,24,128]{3,2,0,1:T(8,128)S(1)}, u32[]{:S(2)}, u32[]{:S(2)}) %collective-permute-start.3) | collective-permute-done | bytes 245792 | tf_op jit(solution)/shard_map/ppermute | solution.py:151
  68.7 42.0 %psum.28 = f32[128,80]{0,1:T(8,128)S(1)} all-reduce(f32[128,80]{0,1:T(8,128)S(1)} %broadcast_select_fusion.3), channel_id=1, replica_groups=mesh['mem'=4,'sub'=8] {'mem','sub'}, use_global_device_ids=true, to_apply=%region_0.1 | all-reduce | flops 10240 | bytes 81920 | tf_op jit(solution)/shard_map/psum | solution.py:169
  111.4 11.7 %cholesky.74 = f32[128,128]{1,0:T(8,128)S(1)} custom-call(f32[128,128]{1,0:T(8,128)S(1)} %copy.43), custom_call_target="Cholesky" | custom-call | tf_op jit(solution)/shard_map/jit(cholesky)/cholesky | solution.py:81
  124.6 9.8 %custom-call.36 = f32[1,128,128]{1,2,0:T(8,128)S(1)} custom-call(f32[1,128,128]{2,1,0:T(8,128)S(1)} %get-tuple-element.25), custom_call_target="InvertDiagBlocksLowerTriangular" | custom-call | tf_op jit(solution)/shard_map/triangular_solve/custom-call.3 | solution.py:88
  134.6 9.8 %custom-call.35 = f32[1,128,128]{1,2,0:T(8,128)S(1)} custom-call(f32[1,128,128]{2,1,0:T(8,128)S(1)} %get-tuple-element.24), custom_call_target="InvertDiagBlocksLowerTriangular" | custom-call | tf_op jit(solution)/shard_map/triangular_solve/custom-call.2 | solution.py:84
  147.8 2.8 fusion.187
  153.1 41.4 %psum.29 = f32[128,80]{0,1:T(8,128)S(1)} all-reduce(f32[128,80]{0,1:T(8,128)S(1)} %broadcast_select_fusion.2), channel_id=1, replica_groups=mesh['mem'=4,'sub'=8] {'mem','sub'}, use_global_device_ids=true, to_apply=%region_5.11 | all-reduce | flops 10240 | bytes 81920 | tf_op jit(solution)/shard_map/psum | solution.py:169
  195.0 11.7 %cholesky.85 = f32[128,128]{1,0:T(8,128)S(1)} custom-call(f32[128,128]{1,0:T(8,128)S(1)} %copy.48), custom_call_target="Cholesky" | custom-call | tf_op jit(solution)/shard_map/jit(cholesky)/cholesky | solution.py:81
  208.0 9.8 %custom-call.40 = f32[1,128,128]{1,2,0:T(8,128)S(1)} custom-call(f32[1,128,128]{2,1,0:T(8,128)S(1)} %get-tuple-element.23), custom_call_target="InvertDiagBlocksLowerTriangular" | custom-call | tf_op jit(solution)/shard_map/triangular_solve/custom-call.3 | solution.py:88
  218.0 9.8 %custom-call.39 = f32[1,128,128]{1,2,0:T(8,128)S(1)} custom-call(f32[1,128,128]{2,1,0:T(8,128)S(1)} %get-tuple-element.22), custom_call_target="InvertDiagBlocksLowerTriangular" | custom-call | tf_op jit(solution)/shard_map/triangular_solve/custom-call.2 | solution.py:84
  228.2 2.6 fusion.37
  235.5 39.5 %psum.30 = f32[128,80]{0,1:T(8,128)S(1)} all-reduce(f32[128,80]{0,1:T(8,128)S(1)} %broadcast_select_fusion.1), channel_id=1, replica_groups=mesh['mem'=4,'sub'=8] {'mem','sub'}, use_global_device_ids=true, to_apply=%region_8.14 | all-reduce | flops 10240 | bytes 81920 | tf_op jit(solution)/shard_map/psum | solution.py:169
  275.5 11.7 %cholesky.96 = f32[128,128]{1,0:T(8,128)S(1)} custom-call(f32[128,128]{1,0:T(8,128)S(1)} %copy.51), custom_call_target="Cholesky" | custom-call | tf_op jit(solution)/shard_map/jit(cholesky)/cholesky | solution.py:81
  288.6 9.8 %custom-call.44 = f32[1,128,128]{1,2,0:T(8,128)S(1)} custom-call(f32[1,128,128]{2,1,0:T(8,128)S(1)} %get-tuple-element.21), custom_call_target="InvertDiagBlocksLowerTriangular" | custom-call | tf_op jit(solution)/shard_map/triangular_solve/custom-call.3 | solution.py:88
  298.6 9.8 %custom-call.43 = f32[1,128,128]{1,2,0:T(8,128)S(1)} custom-call(f32[1,128,128]{2,1,0:T(8,128)S(1)} %get-tuple-element.20), custom_call_target="InvertDiagBlocksLowerTriangular" | custom-call | tf_op jit(solution)/shard_map/triangular_solve/custom-call.2 | solution.py:84
  308.9 2.6 fusion.35
  316.2 41.4 %psum.31 = f32[128,80]{0,1:T(8,128)S(1)} all-reduce(f32[128,80]{0,1:T(8,128)S(1)} %broadcast_select_fusion), channel_id=1, replica_groups=mesh['mem'=4,'sub'=8] {'mem','sub'}, use_global_device_ids=true, to_apply=%region_11.17 | all-reduce | flops 10240 | bytes 81920 | tf_op jit(solution)/shard_map/psum | solution.py:169
  358.1 11.7 %cholesky.107 = f32[128,128]{1,0:T(8,128)S(1)} custom-call(f32[128,128]{1,0:T(8,128)S(1)} %copy.54), custom_call_target="Cholesky" | custom-call | tf_op jit(solution)/shard_map/jit(cholesky)/cholesky | solution.py:81
  371.3 9.8 %custom-call.48 = f32[1,128,128]{1,2,0:T(8,128)S(1)} custom-call(f32[1,128,128]{2,1,0:T(8,128)S(1)} %get-tuple-element.19), custom_call_target="InvertDiagBlocksLowerTriangular" | custom-call | tf_op jit(solution)/shard_map/triangular_solve/custom-call.3 | solution.py:88
  381.3 9.8 %custom-call.47 = f32[1,128,128]{1,2,0:T(8,128)S(1)} custom-call(f32[1,128,128]{2,1,0:T(8,128)S(1)} %get-tuple-element.18), custom_call_target="InvertDiagBlocksLowerTriangular" | custom-call | tf_op jit(solution)/shard_map/triangular_solve/custom-call.2 | solution.py:84
  391.6 2.6 fusion.33
  (166 shorter events, 49.4 us)
Async XLA Ops:
  0.0 15.6 %copy-start.8 = (f32[20,1,24,512]{3,2,1,0:T(8,128)S(1)}, f32[20,1,24,512]{3,2,1,0:T(8,128)}, u32[]{:S(2)}) copy-start(f32[20,1,24,512]{3,2,1,0:T(8,128)} %param.18) | copy-start | bytes 2949124
  0.0 47.4 %collective-permute-start = (f32[20,1,24,512]{3,2,1,0:T(8,128)}, f32[20,1,24,512]{3,2,1,0:T(8,128)}, u32[]{:S(2)}, u32[]{:S(2)}) collective-permute-start(f32[20,1,24,512]{3,2,1,0:T(8,128)} %param.18), channel_id=1, source_target_pairs={{0,1},{1,2},{2,3},{3,4},{4,5},{5,6},{6,7},{8,9},{9,10},{10,11},{11... | collective-permute-start | bytes 2949128 | tf_op jit(solution)/shard_map/ppermute | solution.py:28
  5.9 41.4 %collective-permute-start.1 = (f32[20,1,24,512]{3,2,1,0:T(8,128)}, f32[20,1,24,512]{3,2,1,0:T(8,128)}, u32[]{:S(2)}, u32[]{:S(2)}) collective-permute-start(f32[20,1,24,512]{3,2,1,0:T(8,128)} %param.18), channel_id=1, source_target_pairs={{1,0},{2,1},{3,2},{4,3},{5,4},{6,5},{7,6},{9,8},{10,9},{11,10},{12... | collective-permute-start | bytes 2949128 | tf_op jit(solution)/shard_map/ppermute | solution.py:29
  15.6 31.8 %copy-start.13 = (f32[1,512]{1,0:T(1,128)S(1)}, f32[1,512]{1,0:T(1,128)}, u32[]{:S(2)}) copy-start(f32[1,512]{1,0:T(1,128)} %param.21) | copy-start | bytes 6148
  51.1 8.2 %collective-permute-start.4 = (f32[20,1,24,128]{3,2,0,1:T(8,128)S(1)}, f32[20,1,24,128]{3,2,0,1:T(8,128)S(1)}, u32[]{:S(2)}, u32[]{:S(2)}) collective-permute-start(f32[20,1,24,128]{3,2,0,1:T(8,128)S(1)} %bitcast.355), channel_id=1, source_target_pairs={{0,24},{8,16},{16,8},{24,0},{1,25},{9,17},{17,9},{25,1},{2,26},{10... | collective-permute-start | bytes 737288 | tf_op jit(solution)/shard_map/ppermute | solution.py:151
  51.2 13.4 %collective-permute-start.3 = (f32[20,1,24,128]{3,2,0,1:T(8,128)S(1)}, f32[20,1,24,128]{3,2,0,1:T(8,128)S(1)}, u32[]{:S(2)}, u32[]{:S(2)}) collective-permute-start(f32[20,1,24,128]{3,2,0,1:T(8,128)S(1)} %bitcast.353), channel_id=1, source_target_pairs={{0,16},{8,24},{16,0},{24,8},{1,17},{9,25},{17,1},{25,9},{2,18},{10... | collective-permute-start | bytes 737288 | tf_op jit(solution)/shard_map/ppermute | solution.py:151
  52.7 11.9 %collective-permute-start.2 = (f32[20,1,24,128]{3,2,0,1:T(8,128)S(1)}, f32[20,1,24,128]{3,2,0,1:T(8,128)S(1)}, u32[]{:S(2)}, u32[]{:S(2)}) collective-permute-start(f32[20,1,24,128]{3,2,0,1:T(8,128)S(1)} %bitcast.352), channel_id=1, source_target_pairs={{0,8},{8,0},{16,24},{24,16},{1,9},{9,1},{17,25},{25,17},{2,10},{10... | collective-permute-start | bytes 737288 | tf_op jit(solution)/shard_map/ppermute | solution.py:151
  65.4 0.9 copy-start
  67.1 1.6 copy-start.17
  67.1 43.6 %copy-start.1 = (f32[4,20,24,128]{3,2,1,0:T(8,128)S(1)}, f32[4,20,24,128]{3,2,1,0:T(8,128)}, u32[]{:S(2)}) copy-start(f32[4,20,24,128]{3,2,1,0:T(8,128)} %copy-done) | copy-start | bytes 2949124
  67.2 43.8 %copy-start.25 = (f32[128]{0:T(128)S(1)}, f32[128]{0:T(128)}, u32[]{:S(2)}) copy-start(f32[128]{0:T(128)} %get-tuple-element.56) | copy-start | bytes 1540
  67.2 56.7 %copy-start.24 = (f32[128]{0:T(128)S(1)}, f32[128]{0:T(128)}, u32[]{:S(2)}) copy-start(f32[128]{0:T(128)} %get-tuple-element.53) | copy-start | bytes 1540
  68.6 75.8 %copy-start.11 = (f32[4,128]{1,0:T(4,128)S(1)}, f32[4,128]{1,0:T(4,128)}, u32[]{:S(2)}) copy-start(f32[4,128]{1,0:T(4,128)} %param.23) | copy-start | bytes 6148
  152.4 42.1 %copy-start.23 = (f32[128]{0:T(128)S(1)}, f32[128]{0:T(128)}, u32[]{:S(2)}) copy-start(f32[128]{0:T(128)} %get-tuple-element.55) | copy-start | bytes 1540
  152.4 55.0 %copy-start.22 = (f32[128]{0:T(128)S(1)}, f32[128]{0:T(128)}, u32[]{:S(2)}) copy-start(f32[128]{0:T(128)} %get-tuple-element.52) | copy-start | bytes 1540
  152.4 75.8 %copy-start.10 = (f32[24,128]{1,0:T(8,128)S(1)}, f32[24,128]{1,0:T(8,128)}, u32[]{:S(2)}) copy-start(f32[24,128]{1,0:T(8,128)} %get-tuple-element.68) | copy-start | bytes 36868
  152.4 75.8 %copy-start.5 = (f32[80,24,128]{2,0,1:T(8,128)S(1)}, f32[80,24,128]{2,0,1:T(8,128)}, u32[]{:S(2)}) copy-start(f32[80,24,128]{2,0,1:T(8,128)} %copy-done.4) | copy-start | bytes 2949124
  234.8 40.2 %copy-start.21 = (f32[128]{0:T(128)S(1)}, f32[128]{0:T(128)}, u32[]{:S(2)}) copy-start(f32[128]{0:T(128)} %get-tuple-element.57) | copy-start | bytes 1540
  234.8 53.1 %copy-start.20 = (f32[128]{0:T(128)S(1)}, f32[128]{0:T(128)}, u32[]{:S(2)}) copy-start(f32[128]{0:T(128)} %get-tuple-element.51) | copy-start | bytes 1540
  234.8 74.0 %copy-start.7 = (f32[80,24,128]{2,0,1:T(8,128)S(1)}, f32[80,24,128]{2,0,1:T(8,128)}, u32[]{:S(2)}) copy-start(f32[80,24,128]{2,0,1:T(8,128)} %copy-done.6) | copy-start | bytes 2949124
  315.5 42.1 %copy-start.19 = (f32[128]{0:T(128)S(1)}, f32[128]{0:T(128)}, u32[]{:S(2)}) copy-start(f32[128]{0:T(128)} %get-tuple-element.54) | copy-start | bytes 1540
  315.5 55.1 %copy-start.18 = (f32[128]{0:T(128)S(1)}, f32[128]{0:T(128)}, u32[]{:S(2)}) copy-start(f32[128]{0:T(128)} %get-tuple-element.50) | copy-start | bytes 1540
  315.5 75.7 %copy-start.12 = (f32[4,128]{1,0:T(4,128)S(1)}, f32[4,128]{1,0:T(4,128)}, u32[]{:S(2)}) copy-start(f32[4,128]{1,0:T(4,128)} %param.23) | copy-start | bytes 6148
  315.5 76.0 %copy-start.3 = (f32[80,24,128]{2,0,1:T(8,128)S(1)}, f32[80,24,128]{2,0,1:T(8,128)}, u32[]{:S(2)}) copy-start(f32[80,24,128]{2,0,1:T(8,128)} %copy-done.2) | copy-start | bytes 2949124
  (7 other events, 5.7 us)
